TPU v7x, 256 devices: a whole 4x4x8 slice. The times are simulated.
256 devices in a mesh: col: 8 (over x, core), row: 32 (over y, z).
Axes of the slice: x: 4, y: 4, z: 8, core: 2. Of those that a mesh axis runs over, the one named last changes fastest.
Arguments:
- features: float32 [32768, 512], P(('row', 'col')), may hold values from -6 to 6
- weight: float32 [512, 512], replicated, may hold values from -0.25 to 0.25
- tiles: bfloat16 [8, 32, 48, 128, 128], P('col', 'row'), may hold values from -0.09375 to 0.09375
- tile_rows: int32 [8, 32, 48], P('col', 'row'), may hold values from 0 to 31, as said below
- tile_cols: int32 [8, 32, 48], P('col', 'row'), may hold values from 0 to 7
- tile_count: int32 [8, 32], P('col', 'row'), may hold values from 1 to 48, as said below
- cotangent: bfloat16 [32768, 512], P(('col', 'row')), may hold values from -6 to 6
Outputs:
- aggregated: bfloat16 [32768, 512], P(('col', 'row'))
- grad_x: float32 [32768, 512], P(('row', 'col'))
- grad_w: float32 [512, 512], replicated
Inputs may be any that keep to these rules, and one draw needn't show every extreme that they name: `tile_rows`: within one grid block the live slots name distinct tiles. `tile_count`: some grid block has all 48 slots live.
All inputs are finite; a program needn't handle non-finite values.
Results may differ from a plain program's by a relative error of at most 0.0049.
Values may be sent and summed in bfloat16 or wider, within the bound.
No kernel may reach another device: no remote copies, remote signals or barrier semaphores. Data moves between devices by JAX's collectives and lax.ppermute only.
A program may use at most 128 MiB of HBM per device.

v0:
```python
import jax
import jax.numpy as jnp
from jax import lax
from jax.sharding import PartitionSpec as P


def shards(features, weight, tiles, tile_rows, tile_cols, tile_count, cotangent):
    tile_size = tiles.shape[-1]
    slot_count = tiles.shape[2]
    feat_width = features.shape[1]
    blocks = tiles[0, 0]
    rows_idx = tile_rows[0, 0]
    cols_idx = tile_cols[0, 0]
    live_slots = jnp.arange(slot_count, dtype=jnp.int32) < tile_count[0, 0]
    local_rows = jnp.dot(
        features, weight, precision=lax.Precision.HIGHEST, preferred_element_type=jnp.float32
    ).astype(jnp.bfloat16)
    source = lax.all_gather(local_rows, "col", axis=0, tiled=True)
    source_tiles = source.reshape(-1, tile_size, feat_width)
    src_count = source_tiles.shape[0]
    out_tiles = lax.axis_size("row") * features.shape[0] // tile_size
    picked = jnp.take(source_tiles, cols_idx, axis=0)
    tile_terms = jnp.einsum("tab,tbf->taf", blocks, picked, preferred_element_type=jnp.float32)
    select_dst = (
        (rows_idx[None, :] == jnp.arange(out_tiles, dtype=jnp.int32)[:, None]) & live_slots[None, :]
    ).astype(jnp.float32)
    partial_value = jnp.einsum(
        "it,taf->iaf", select_dst, tile_terms, precision=lax.Precision.HIGHEST
    )
    partial_value = partial_value.reshape(out_tiles * tile_size, feat_width)
    aggregated = lax.psum_scatter(partial_value, "row", scatter_dimension=0, tiled=True).astype(
        jnp.bfloat16
    )
    gathered = lax.all_gather(cotangent, "row", axis=0, tiled=True)
    grad_tiles = gathered.reshape(out_tiles, tile_size, feat_width)
    picked_grad = jnp.take(grad_tiles, rows_idx, axis=0)
    back_terms = jnp.einsum("tab,taf->tbf", blocks, picked_grad, preferred_element_type=jnp.float32)
    select_src = (
        (cols_idx[None, :] == jnp.arange(src_count, dtype=jnp.int32)[:, None]) & live_slots[None, :]
    ).astype(jnp.float32)
    back_partial = jnp.einsum(
        "kt,tbf->kbf", select_src, back_terms, precision=lax.Precision.HIGHEST
    )
    back_partial = back_partial.reshape(src_count * tile_size, feat_width)
    grad_y = lax.psum_scatter(back_partial, "col", scatter_dimension=0, tiled=True)
    grad_x = jnp.dot(
        grad_y, weight.T, precision=lax.Precision.HIGHEST, preferred_element_type=jnp.float32
    )
    weight_terms = jnp.dot(
        features.T, grad_y, precision=lax.Precision.HIGHEST, preferred_element_type=jnp.float32
    )
    grad_w = lax.psum(weight_terms, ("col", "row"))
    return (aggregated, grad_x, grad_w)


def solution(mesh):
    placed = (
        P(("row", "col"), None),
        P(),
        P("col", "row", None, None, None),
        P("col", "row", None),
        P("col", "row", None),
        P("col", "row"),
        P(("col", "row"), None),
    )
    return jax.shard_map(
        shards,
        mesh=mesh,
        in_specs=placed,
        out_specs=(P(("col", "row"), None), P(("row", "col"), None), P()),
        check_vma=False,
    )
```

profile of v0, /device:TPU:2, one launch (start us, length us, event | category | flops | bytes accessed | tf_op | source)
XLA Modules:
  0.0 670.1 jit_solution(10211312557095690399)
XLA Ops:
  7.2 0.0 all-gather.5.cloned.1.call-start
  7.2 0.7 all-gather.5.cloned.1.call-update
  7.9 0.0 all-gather.3.cloned.1.call-start
  8.0 2.7 convolution_convert_fusion
  10.6 0.0 all-gather.3.cloned.1.call-update
  10.7 0.0 reduce-scatter.5.cloned.1.call-start
  10.7 0.7 fusion.25
  12.1 0.7 compare_and_fusion
  12.7 82.7 %all-gather.5.cloned.1.call-done = bf16[4096,512]{1,0:T(8,128)(2,1)} async-done(((bf16[128,512]{1,0:T(8,128)(2,1)}), bf16[4096,512]{1,0:T(8,128)(2,1)}) %all-gather.5.cloned.1.call-update) | async-done | bytes 4194320 | tf_op jit(solution)/shard_map/all_gather | solution.py:34
  95.4 7.1 %gather_fusion.1 = bf16[48,128,512]{2,1,0:T(8,128)(2,1)} fusion(bf16[32,128,512]{2,1,0:T(8,128)(2,1)} %bitcast.45, s32[1024]{0:T(1024)S(1)} %pad_clamp_fusion), kind=kCustom, calls=%fused_computation.1 | custom fusion | bytes 12583104 | tf_op jit(solution)/shard_map/jit(_take)/gather | solution.py:36
  102.5 9.2 %fusion.4 = f32[48,512,128]{2,1,0:T(8,128)} fusion(bf16[48,128,512]{2,1,0:T(8,128)(2,1)} %gather_fusion.1, pred[48]{0:T(512)(128)(4,1)S(1)} %compare_and_fusion, bf16[1,1,48,128,128]{4,3,2,1,0:T(8,128)(2,1)S(1)} %copy-done), kind=kOutput, calls=%fused_computation.6 | convolution fusion | flops 808452096 | bytes 20447280 | tf_op jit(solution)/shard_map/tab,taf->tbf/dot_general | solution.py:37
  111.7 12.7 %copy.15 = f32[48,512,128]{1,0,2:T(8,128)} copy(f32[48,512,128]{2,1,0:T(8,128)} %fusion.4) | data formatting | bytes 25165824 | tf_op jit(solution)/shard_map/tab,taf->tbf/dot_general | solution.py:37
  124.4 8.2 %fusion = f32[8,128,512]{2,0,1:T(8,128)S(1)} fusion(f32[48,512,128]{1,0,2:T(8,128)} %copy.15, s32[48]{0:T(128)S(1)} %bitcast.47, pred[48]{0:T(512)(128)(4,1)S(1)} %iota_compare_fusion.2), kind=kOutput, calls=%fused_computation.2 | convolution fusion | flops 301990656 | bytes 14680304 | tf_op jit(solution)/shard_map/kt,tbf->kbf/dot_general | solution.py:41
  132.6 2.6 copy.12
  135.2 0.0 reduce-scatter.5.cloned.1.call-update
  135.2 0.2 all-reduce.2.cloned.1.call-start
  135.5 0.0 all-gather.3.cloned.1.call-done
  135.5 6.2 gather_fusion
  141.7 9.4 %fusion.6 = f32[48,512,128]{2,1,0:T(8,128)} fusion(bf16[48,128,512]{2,1,0:T(8,128)(2,1)} %gather_fusion, pred[48]{0:T(512)(128)(4,1)S(1)} %compare_and_fusion.1, bf16[1,1,48,128,128]{4,3,2,1,0:T(8,128)(2,1)S(1)} %copy-done), kind=kOutput, calls=%fused_computation.8 | convolution fusion | flops 808452096 | bytes 20447280 | tf_op jit(solution)/shard_map/tab,tbf->taf/dot_general | solution.py:23
  151.1 12.9 %copy.14 = f32[48,512,128]{1,0,2:T(8,128)} copy(f32[48,512,128]{2,1,0:T(8,128)} %fusion.6) | data formatting | bytes 25165824 | tf_op jit(solution)/shard_map/tab,tbf->taf/dot_general | solution.py:23
  164.0 1.5 reduce-scatter.5.cloned.1.call-done
  165.5 2.9 convolution_bitcast_fusion
  168.4 0.0 reduce-scatter.3.cloned.1.call-start
  168.5 14.4 %fusion.2 = f32[32,128,512]{2,0,1:T(8,128)S(1)} fusion(f32[48,512,128]{1,0,2:T(8,128)} %copy.14, s32[48]{0:T(128)S(1)} %bitcast.48, pred[48]{0:T(512)(128)(4,1)S(1)} %iota_compare_fusion.2), kind=kOutput, calls=%fused_computation.4 | convolution fusion | flops 1207962624 | bytes 20971760 | tf_op jit(solution)/shard_map/it,taf->iaf/dot_general | solution.py:27
  183.0 8.1 %copy.11 = f32[32,128,512]{2,1,0:T(8,128)} copy(f32[32,128,512]{2,0,1:T(8,128)S(1)} %fusion.2) | data formatting | bytes 16777216 | tf_op jit(solution)/shard_map/it,taf->iaf/dot_general | solution.py:27
  191.1 1.2 copy-done.2
  192.3 0.0 copy-done.4
  192.3 1.9 fusion.28
  194.2 235.5 %all-reduce.2.cloned.1.call-done = f32[512,512]{0,1:T(8,128)} async-done(((f32[512,512]{0,1:T(8,128)}), f32[512,512]{0,1:T(8,128)}) %all-reduce.2.cloned.1.call-update) | async-done | bytes 1048592 | tf_op jit(solution)/shard_map/psum | solution.py:52
  429.7 2.5 copy.13
  432.2 229.7 %reduce-scatter.3.cloned.1.call-done = f32[128,512]{1,0:T(8,128)} async-done(((f32[4096,512]{1,0:T(8,128)}), f32[128,512]{1,0:T(8,128)}) %reduce-scatter.3.cloned.1.call-update) | async-done | bytes 262160 | tf_op jit(solution)/shard_map/reduce_scatter | solution.py:31
  661.9 1.6 convert_element_type.9
  (19 shorter events, 0.1 us)
Async XLA Ops:
  7.2 95.3 %copy-start = (bf16[1,1,48,128,128]{4,3,2,1,0:T(8,128)(2,1)S(1)}, bf16[1,1,48,128,128]{4,3,2,1,0:T(8,128)(2,1)}, u32[]{:S(2)}) copy-start(bf16[1,1,48,128,128]{4,3,2,1,0:T(8,128)(2,1)} %param.9) | copy-start | bytes 4718596
  7.2 88.2 %all-gather.5.cloned.1.call-start = ((), (), s32[]{:S(2)}) async-start(), calls=%async_computation.4 | async-start | bytes 4325376 | tf_op jit(solution)/shard_map/all_gather | solution.py:34
  7.9 127.6 %all-gather.3.cloned.1.call-start = ((), (), s32[]{:S(2)}) async-start(), calls=%async_computation.2 | async-start | bytes 1179648 | tf_op jit(solution)/shard_map/all_gather | solution.py:18
  10.7 154.8 %reduce-scatter.5.cloned.1.call-start = ((), (), s32[]{:S(2)}) async-start(), calls=%async_computation.5 | async-start | bytes 2359296 | tf_op jit(solution)/shard_map/reduce_scatter | solution.py:45
  111.7 12.8 %copy-start.5 = (s32[1,1,48]{2,1,0:T(1,128)S(1)}, s32[1,1,48]{2,1,0:T(1,128)}, u32[]{:S(2)}) copy-start(s32[1,1,48]{2,1,0:T(1,128)} %param.11) | copy-start | bytes 580
  135.2 294.5 %all-reduce.2.cloned.1.call-start = ((), (), s32[]{:S(2)}) async-start(), calls=%async_computation.6 | async-start | bytes 2097152 | tf_op jit(solution)/shard_map/psum | solution.py:52
  151.0 14.4 %copy-start.3 = (f32[128,512]{1,0:T(8,128)S(1)}, f32[128,512]{1,0:T(8,128)}, u32[]{:S(2)}) copy-start(f32[128,512]{1,0:T(8,128)} %param.7) | copy-start | bytes 786436
  151.0 17.4 %copy-start.6 = (s32[1,1,48]{2,1,0:T(1,128)S(1)}, s32[1,1,48]{2,1,0:T(1,128)}, u32[]{:S(2)}) copy-start(s32[1,1,48]{2,1,0:T(1,128)} %param.10) | copy-start | bytes 580
  168.4 493.5 %reduce-scatter.3.cloned.1.call-start = ((), (), s32[]{:S(2)}) async-start(), calls=%async_computation.3 | async-start | bytes 8650752 | tf_op jit(solution)/shard_map/reduce_scatter | solution.py:31
  183.0 480.6 %copy-start.1 = (bf16[1,1,48,128,128]{4,3,2,1,0:T(8,128)(2,1)S(1)}, bf16[1,1,48,128,128]{4,3,2,1,0:T(8,128)(2,1)}, u32[]{:S(2)}) copy-start(bf16[1,1,48,128,128]{4,3,2,1,0:T(8,128)(2,1)} %param.9) | copy-start | bytes 4718596
  191.1 1.2 copy-start.2
  191.1 1.3 copy-start.4
Sparse Core Ops, SparseCore 0:
  10.6 84.7 all-gather.4
  97.8 21.4 all-gather.2
  135.3 30.0 reduce-scatter.4
  171.3 258.3 all-reduce.1
  434.1 227.7 reduce-scatter.2
where the time goes:
time: 671 us; the launch traced here: 670 us
  waiting for transfers between devices  550 us (82%)
  local copies, waits for them, and re-layouts  53.4 us (8%)
  matrix products  48.7 us (7%)
  between operations  14.5 us (2%)
    psum x1, waiting for transfers between devices, shards(): grad_w = lax.psum(weight_terms, ('col', 'row'))  235 us
    reduce_scatter x1, waiting for transfers between devices, shards(): lax.psum_scatter(partial_value, 'row', scatter_dimension=0, tiled=True)  230 us
    all_gather x1, waiting for transfers between devices, shards(): gathered = lax.all_gather(cotangent, 'row', axis=0, tiled=True)  82.7 us
    dot_general x1, matrix products, shards(): jnp.einsum('it,taf->iaf', select_dst, tile_terms, precision=lax.Precision...  14.4 us
  transfers between devices with their start and end apart: 5, of which 4 were waited for; matrix products, arithmetic and copies ran while one was open for 15% of the time, Pallas kernels for 0%

commit v1 on v0

--- a/solution.py
+++ b/solution.py
@@ -31,7 +31,8 @@
     aggregated = lax.psum_scatter(partial_value, "row", scatter_dimension=0, tiled=True).astype(
         jnp.bfloat16
     )
-    gathered = lax.all_gather(cotangent, "row", axis=0, tiled=True)
+    stack = jnp.stack([cotangent] * lax.axis_size("row"))
+    gathered = jnp.concatenate(lax.all_to_all(stack, "row", 0, 0), axis=0)
     grad_tiles = gathered.reshape(out_tiles, tile_size, feat_width)
     picked_grad = jnp.take(grad_tiles, rows_idx, axis=0)
     back_terms = jnp.einsum("tab,taf->tbf", blocks, picked_grad, preferred_element_type=jnp.float32)

time: 671 us -> 694 us (1.034)
  starting transfers between devices: 0.38 us -> 12 us
  waiting for transfers between devices: 550 us -> 561 us
    all_to_all x0 -> x1, waiting for transfers between devices: none -> 95 us  [shards(): gathered = jnp.concatenate(lax.all_to_all(stack, 'row', 0, 0), axis=0)]
    all_gather x1 -> x0, waiting for transfers between devices: 82.7 us -> none  [shards(): gathered = lax.all_gather(cotangent, 'row', axis=0, tiled=True)]
    all_to_all x0 -> x1, starting transfers between devices: none -> 11.6 us  [shards(): gathered = jnp.concatenate(lax.all_to_all(stack, 'row', 0, 0), axis=0)]
  transfers between devices with their start and end apart: 5 -> 5, of which waited for: 4 -> 4; matrix products, arithmetic and copies ran while one was open for 15% -> 14% of each run, Pallas kernels for 0% -> 0%
where the time goes in v1:
time: 694 us; the launch traced here: 693 us
  waiting for transfers between devices  561 us (81%)
  local copies, waits for them, and re-layouts  56.5 us (8%)
  matrix products  47.5 us (7%)
  between operations  14.6 us (2%)
  starting transfers between devices  12 us (2%)
    psum x1, waiting for transfers between devices, shards(): grad_w = lax.psum(weight_terms, ('col', 'row'))  236 us
    reduce_scatter x1, waiting for transfers between devices, shards(): lax.psum_scatter(partial_value, 'row', scatter_dimension=0, tiled=True)  230 us
    all_to_all x1, waiting for transfers between devices, shards(): gathered = jnp.concatenate(lax.all_to_all(stack, 'row', 0, 0), axis=0)  95 us
    dot_general x1, matrix products, shards(): jnp.einsum('it,taf->iaf', select_dst, tile_terms, precision=lax.Precision...  14.4 us
  transfers between devices with their start and end apart: 5, of which 4 were waited for; matrix products, arithmetic and copies ran while one was open for 14% of the time, Pallas kernels for 0%

profile of v1, /device:TPU:2, one launch (start us, length us, event | category | flops | bytes accessed | tf_op | source)
XLA Modules:
  0.0 693.4 jit_solution(15520990876580063290)
XLA Ops:
  7.2 0.0 copy-start
  7.2 3.5 stack.2
  10.7 11.6 %all-to-all-start = ((bf16[32,128,512]{2,1,0:T(8,128)(2,1)}), bf16[32,128,512]{2,1,0:T(8,128)(2,1)}, u32[]{:S(2)}, u32[]{:S(2)}) async-start(bf16[32,128,512]{2,1,0:T(8,128)(2,1)} %stack.2), calls=%async_computation.1 | async-start | bytes 8388608 | tf_op jit(solution)/shard_map/all_to_all | solution.py:35
  22.3 0.0 all-gather.2.cloned.1.call-start
  22.4 1.4 convolution_convert_fusion
  23.8 0.0 all-gather.2.cloned.1.call-update
  23.8 0.0 reduce-scatter.5.cloned.1.call-start
  24.5 95.0 %all-to-all-done = bf16[32,128,512]{2,1,0:T(8,128)(2,1)} async-done(((bf16[32,128,512]{2,1,0:T(8,128)(2,1)}), bf16[32,128,512]{2,1,0:T(8,128)(2,1)}, u32[]{:S(2)}, u32[]{:S(2)}) %all-to-all-start) | async-done | bytes 4194336 | tf_op jit(solution)/shard_map/all_to_all | solution.py:35
  119.5 7.1 %gather_fusion.1 = bf16[48,128,512]{2,1,0:T(8,128)(2,1)} fusion(bf16[32,128,512]{2,1,0:T(8,128)(2,1)} %all-to-all-done, s32[1024]{0:T(1024)S(1)} %pad_clamp_fusion), kind=kCustom, calls=%fused_computation.1 | custom fusion | bytes 12583104 | tf_op jit(solution)/shard_map/jit(_take)/gather | solution.py:37
  126.6 9.2 %fusion.4 = f32[48,512,128]{2,1,0:T(8,128)} fusion(bf16[48,128,512]{2,1,0:T(8,128)(2,1)} %gather_fusion.1, pred[48]{0:T(512)(128)(4,1)S(1)} %compare_and_fusion, bf16[1,1,48,128,128]{4,3,2,1,0:T(8,128)(2,1)S(1)} %copy-done), kind=kOutput, calls=%fused_computation.6 | convolution fusion | flops 808452096 | bytes 20447280 | tf_op jit(solution)/shard_map/tab,taf->tbf/dot_general | solution.py:38
  135.8 12.8 %copy.15 = f32[48,512,128]{1,0,2:T(8,128)} copy(f32[48,512,128]{2,1,0:T(8,128)} %fusion.4) | data formatting | bytes 25165824 | tf_op jit(solution)/shard_map/tab,taf->tbf/dot_general | solution.py:38
  148.6 8.2 %fusion = f32[8,128,512]{2,0,1:T(8,128)S(1)} fusion(f32[48,512,128]{1,0,2:T(8,128)} %copy.15, s32[48]{0:T(128)S(1)} %bitcast.45, pred[48]{0:T(512)(128)(4,1)S(1)} %iota_compare_fusion.2), kind=kOutput, calls=%fused_computation.2 | convolution fusion | flops 301990656 | bytes 14680304 | tf_op jit(solution)/shard_map/kt,tbf->kbf/dot_general | solution.py:42
  156.8 2.6 copy.12
  159.4 0.0 reduce-scatter.5.cloned.1.call-update
  159.4 0.2 all-reduce.2.cloned.1.call-start
  159.7 0.0 all-gather.2.cloned.1.call-done
  159.7 6.2 gather_fusion
  165.9 9.4 %fusion.6 = f32[48,512,128]{2,1,0:T(8,128)} fusion(bf16[48,128,512]{2,1,0:T(8,128)(2,1)} %gather_fusion, pred[48]{0:T(512)(128)(4,1)S(1)} %compare_and_fusion.1, bf16[1,1,48,128,128]{4,3,2,1,0:T(8,128)(2,1)S(1)} %copy-done), kind=kOutput, calls=%fused_computation.8 | convolution fusion | flops 808452096 | bytes 20447280 | tf_op jit(solution)/shard_map/tab,tbf->taf/dot_general | solution.py:23
  175.3 12.8 %copy.14 = f32[48,512,128]{1,0,2:T(8,128)} copy(f32[48,512,128]{2,1,0:T(8,128)} %fusion.6) | data formatting | bytes 25165824 | tf_op jit(solution)/shard_map/tab,tbf->taf/dot_general | solution.py:23
  188.1 0.8 reduce-scatter.5.cloned.1.call-done
  188.9 2.9 convolution_bitcast_fusion
  191.8 0.0 all-reduce.2.cloned.1.call-update
  191.8 0.0 reduce-scatter.3.cloned.1.call-start
  191.9 14.4 %fusion.2 = f32[32,128,512]{2,0,1:T(8,128)S(1)} fusion(f32[48,512,128]{1,0,2:T(8,128)} %copy.14, s32[48]{0:T(128)S(1)} %bitcast.46, pred[48]{0:T(512)(128)(4,1)S(1)} %iota_compare_fusion.2), kind=kOutput, calls=%fused_computation.4 | convolution fusion | flops 1207962624 | bytes 20971760 | tf_op jit(solution)/shard_map/it,taf->iaf/dot_general | solution.py:27
  206.3 8.1 %copy.11 = f32[32,128,512]{2,1,0:T(8,128)} copy(f32[32,128,512]{2,0,1:T(8,128)S(1)} %fusion.2) | data formatting | bytes 16777216 | tf_op jit(solution)/shard_map/it,taf->iaf/dot_general | solution.py:27
  214.4 0.0 reduce-scatter.3.cloned.1.call-update
  214.4 0.9 copy-done.4
  215.4 1.9 fusion.28
  217.2 235.7 %all-reduce.2.cloned.1.call-done = f32[512,512]{0,1:T(8,128)} async-done(((f32[512,512]{0,1:T(8,128)}), f32[512,512]{0,1:T(8,128)}) %all-reduce.2.cloned.1.call-update) | async-done | bytes 1048592 | tf_op jit(solution)/shard_map/psum | solution.py:53
  453.0 2.5 copy.13
  455.5 229.8 %reduce-scatter.3.cloned.1.call-done = f32[128,512]{1,0:T(8,128)} async-done(((f32[4096,512]{1,0:T(8,128)}), f32[128,512]{1,0:T(8,128)}) %reduce-scatter.3.cloned.1.call-update) | async-done | bytes 262160 | tf_op jit(solution)/shard_map/reduce_scatter | solution.py:31
  685.3 1.6 convert_element_type.9
  (19 shorter events, 0.1 us)
Async XLA Ops:
  7.2 119.4 %copy-start = (bf16[1,1,48,128,128]{4,3,2,1,0:T(8,128)(2,1)S(1)}, bf16[1,1,48,128,128]{4,3,2,1,0:T(8,128)(2,1)}, u32[]{:S(2)}) copy-start(bf16[1,1,48,128,128]{4,3,2,1,0:T(8,128)(2,1)} %param.9) | copy-start | bytes 4718596
  7.2 15.2 %copy-start.3 = (f32[128,512]{1,0:T(8,128)S(1)}, f32[128,512]{1,0:T(8,128)}, u32[]{:S(2)}) copy-start(f32[128,512]{1,0:T(8,128)} %param.7) | copy-start | bytes 786436
  7.2 15.2 %copy-start.2 = (f32[512,512]{1,0:T(8,128)S(1)}, f32[512,512]{1,0:T(8,128)}, u32[]{:S(2)}) copy-start(f32[512,512]{1,0:T(8,128)} %param.8) | copy-start | bytes 3145732
  7.2 16.6 %copy-start.6 = (s32[1,1,48]{2,1,0:T(1,128)S(1)}, s32[1,1,48]{2,1,0:T(1,128)}, u32[]{:S(2)}) copy-start(s32[1,1,48]{2,1,0:T(1,128)} %param.10) | copy-start | bytes 580
  10.7 108.8 %all-to-all-start = ((bf16[32,128,512]{2,1,0:T(8,128)(2,1)}), bf16[32,128,512]{2,1,0:T(8,128)(2,1)}, u32[]{:S(2)}, u32[]{:S(2)}) async-start(bf16[32,128,512]{2,1,0:T(8,128)(2,1)} %stack.2), calls=%async_computation.1 | async-start | bytes 8388608 | tf_op jit(solution)/shard_map/all_to_all | solution.py:35
  22.3 137.4 %all-gather.2.cloned.1.call-start = ((), (), s32[]{:S(2)}) async-start(), calls=%async_computation.3 | async-start | bytes 1179648 | tf_op jit(solution)/shard_map/all_gather | solution.py:18
  23.8 165.1 %reduce-scatter.5.cloned.1.call-start = ((), (), s32[]{:S(2)}) async-start(), calls=%async_computation.5 | async-start | bytes 2359296 | tf_op jit(solution)/shard_map/reduce_scatter | solution.py:46
  135.8 12.8 %copy-start.5 = (s32[1,1,48]{2,1,0:T(1,128)S(1)}, s32[1,1,48]{2,1,0:T(1,128)}, u32[]{:S(2)}) copy-start(s32[1,1,48]{2,1,0:T(1,128)} %param.11) | copy-start | bytes 580
  159.4 293.6 %all-reduce.2.cloned.1.call-start = ((), (), s32[]{:S(2)}) async-start(), calls=%async_computation.6 | async-start | bytes 2097152 | tf_op jit(solution)/shard_map/psum | solution.py:53
  191.8 493.4 %reduce-scatter.3.cloned.1.call-start = ((), (), s32[]{:S(2)}) async-start(), calls=%async_computation.4 | async-start | bytes 8650752 | tf_op jit(solution)/shard_map/reduce_scatter | solution.py:31
  206.3 480.6 %copy-start.1 = (bf16[1,1,48,128,128]{4,3,2,1,0:T(8,128)(2,1)S(1)}, bf16[1,1,48,128,128]{4,3,2,1,0:T(8,128)(2,1)}, u32[]{:S(2)}) copy-start(bf16[1,1,48,128,128]{4,3,2,1,0:T(8,128)(2,1)} %param.9) | copy-start | bytes 4718596
  214.4 0.9 copy-start.4
Sparse Core Ops, SparseCore 0:
  25.6 25.3 all-gather.1
  159.5 29.2 reduce-scatter.4
  194.9 258.0 all-reduce.1
  457.4 227.8 reduce-scatter.2
